TPU v7x, 32 devices: a whole 2x2x4 slice. The times are simulated.
32 devices in a mesh: kern: 8 (over y, x, core), fac: 2 (over z_hi), pair: 2 (over z_lo).
Axes of the slice: x: 2, y: 2, z: 4 (z_hi: 2, z_lo: 2; z = z_hi * 2 + z_lo), core: 2. Of those that a mesh axis runs over, the one named last changes fastest.
Arguments:
- points: bfloat16 [32768, 3072], P('kern', ('fac', 'pair')), may hold values from -6 to 6
- factor: float32 [32768, 3072], P(('kern', 'fac', 'pair')), may hold values from -0.02690478 to 0.02690478
- panel_block: int32 [1], replicated, may hold values from 0 to 63
- finished: int32 [1], replicated, may hold values from 1536 to 3072
Outputs:
- panel_factor: float32 [32768, 512], P(('kern', 'fac', 'pair'))
Inputs may be any that keep to these rules, and one draw needn't show every extreme that they name: The panel's points are rows 512 * panel_block to 512 * panel_block + 511. Columns of factor from finished on are not used.
All inputs are finite; a program needn't handle non-finite values.
Results may differ from a plain program's by a relative error of at most 0.0006.
Values may be sent and summed in bfloat16 or wider, within the bound.
No kernel may reach another device: no remote copies, remote signals or barrier semaphores. Data moves between devices by JAX's collectives and lax.ppermute only.
A program may use at most 128 MiB of HBM per device.

v0:
```python
import jax
import jax.numpy as jnp
from jax import lax
from jax.sharding import PartitionSpec as P

DIN = 3072
P_SIZE = 512
LAYERS = 5
RIDGE = 3.0
EPS = 1e-06


def from_root(shard, axis, root):
    mine = lax.axis_index(axis) == root
    return lax.psum(jnp.where(mine, shard, jnp.zeros_like(shard)), axis)


def tangent_kernel(products, left_norm, right_norm):
    scales = jnp.sqrt(left_norm * right_norm)
    covariance = products
    tangent = products
    for repeat in range(LAYERS):
        cosine = jnp.clip(covariance / scales, -1.0, 1.0)
        angles = jnp.arccos(cosine)
        covariance = scales * (jnp.sin(angles) + (jnp.pi - angles) * cosine) / jnp.pi
        slopes = (jnp.pi - angles) / jnp.pi
        tangent = covariance + slopes * tangent
    return tangent


def body(points, factor, panel_block, finished):
    kern_rows = points.shape[0]
    own_rows = factor.shape[0]
    group_size = lax.axis_size(("fac", "pair"))
    position = lax.axis_index(("fac", "pair"))
    kern_index = lax.axis_index("kern")
    panel_start = panel_block[0] * P_SIZE
    used_count = finished[0]
    root_kern = panel_start // kern_rows
    local_points = lax.dynamic_slice_in_dim(points, panel_start - root_kern * kern_rows, P_SIZE, 0)
    panel_points = from_root(local_points, "kern", root_kern)
    owner_index = panel_start // own_rows
    local_rows = lax.dynamic_slice_in_dim(factor, panel_start - owner_index * own_rows, P_SIZE, 0)
    panel_rows = from_root(
        local_rows.astype(jnp.bfloat16), ("kern", "fac", "pair"), owner_index
    ).astype(local_rows.dtype)
    column_keep = (jnp.arange(factor.shape[1], dtype=jnp.int32) < used_count).astype(jnp.float32)
    panel_rows = panel_rows * column_keep[None, :]
    panel_part = jnp.sum(jnp.square(panel_points.astype(jnp.float32)), axis=1)
    pair_part = lax.dot_general(
        panel_points, panel_points, (((1,), (1,)), ((), ())), preferred_element_type=jnp.float32
    )
    pair_sum, panel_sum = lax.psum((pair_part, panel_part), ("fac", "pair"))
    panel_norm = panel_sum / DIN + EPS
    row_part = jnp.sum(jnp.square(points.astype(jnp.float32)), axis=1)
    inner_part = lax.dot_general(
        points, panel_points, (((1,), (1,)), ((), ())), preferred_element_type=jnp.float32
    )
    inner_rows, row_sum = (
        lax.psum_scatter(inner_part, ("fac", "pair"), scatter_dimension=0, tiled=True),
        lax.psum_scatter(row_part, ("fac", "pair"), scatter_dimension=0, tiled=True),
    )
    kernel = tangent_kernel(inner_rows / DIN, (row_sum / DIN + EPS)[:, None], panel_norm[None, :])
    row_index = (kern_index * group_size + position) * own_rows + jnp.arange(
        own_rows, dtype=jnp.int32
    )
    col_index = jnp.arange(P_SIZE, dtype=jnp.int32)
    kernel = jnp.where(
        row_index[:, None] == panel_start + col_index[None, :], kernel + RIDGE, kernel
    )
    updated = kernel - jnp.dot(
        factor, panel_rows.T, precision=lax.Precision.HIGHEST, preferred_element_type=jnp.float32
    )
    diag_kernel = tangent_kernel(pair_sum / DIN, panel_norm[:, None], panel_norm[None, :])
    diag_index = jnp.arange(P_SIZE, dtype=jnp.int32)
    diag_kernel = jnp.where(
        diag_index[:, None] == diag_index[None, :], diag_kernel + RIDGE, diag_kernel
    )
    diag_block = diag_kernel - jnp.dot(
        panel_rows,
        panel_rows.T,
        precision=lax.Precision.HIGHEST,
        preferred_element_type=jnp.float32,
    )
    lower_factor = jnp.linalg.cholesky(diag_block)
    return lax.linalg.triangular_solve(
        lower_factor, updated, left_side=False, lower=True, transpose_a=True
    )


def solution(mesh):
    placed = (P("kern", ("fac", "pair")), P(("kern", "fac", "pair"), None), P(), P())
    return jax.shard_map(
        body,
        mesh=mesh,
        in_specs=placed,
        out_specs=P(("kern", "fac", "pair"), None),
        check_vma=False,
    )
```

profile of v0, /device:TPU:0, one launch (start us, length us, event | category | flops | bytes accessed | tf_op | source)
XLA Modules:
  0.0 541.0 jit_solution(6389114179767926636)
XLA Ops:
  7.2 2.1 dynamic-slice_select_fusion
  9.4 0.0 all-reduce.7.cloned.1.call-update
  9.4 0.0 all-reduce.11.cloned.1.call-start
  9.4 59.5 %all-reduce.7.cloned.1.call-done = bf16[512,768]{1,0:T(8,128)(2,1)} async-done(((bf16[512,768]{1,0:T(8,128)(2,1)}), bf16[512,768]{1,0:T(8,128)(2,1)}) %all-reduce.7.cloned.1.call-update) | async-done | bytes 786448 | tf_op jit(solution)/shard_map/psum | solution.py:15
  68.9 2.9 fusion.44
  71.8 0.0 all-reduce.11.cloned.1.call-update
  71.9 0.0 all-reduce.9.cloned.1.call-start
  72.0 5.3 fusion.2
  77.2 0.0 all-reduce.9.cloned.1.call-update
  77.3 0.0 reduce-scatter.2.cloned.1.call-start
  77.3 1.1 copy-done
  78.4 8.4 %convolution_bitcast_fusion = f32[4096,512]{0,1:T(8,128)} fusion(bf16[512,768]{1,0:T(8,128)(2,1)S(1)} %copy-done, bf16[4096,768]{1,0:T(8,128)(2,1)} %param.4), kind=kOutput, calls=%fused_computation.3 | convolution fusion | flops 3221225472 | bytes 15466496 | tf_op jit(solution)/shard_map/dot_general | solution.py:56
  87.5 0.7 dynamic-slice.3
  88.9 4.1 multiply_reduce_fusion
  93.0 0.2 multiply_reduce_fusion.1
  93.2 19.6 %all-reduce.2 = (f32[512]{0:T(512)S(1)}, f32[4096]{0:T(1024)S(1)}) all-reduce(f32[512]{0:T(512)S(1)} %multiply_reduce_fusion.1, f32[4096]{0:T(1024)S(1)} %multiply_reduce_fusion), channel_id=1, replica_groups=mesh['kern'=8,'fac'=2,'pair'=2] {'fac','pair'}, use_global_device_ids=true, to_apply=%region_4.5 | all-reduce | flops 4608 | bytes 36864 | tf_op jit(solution)/shard_map/psum | solution.py:53
  112.8 10.6 %all-reduce.11.cloned.1.call-done = f32[512,512]{0,1:T(8,128)} async-done(((f32[512,512]{0,1:T(8,128)}), f32[512,512]{0,1:T(8,128)}) %all-reduce.11.cloned.1.call-update) | async-done | bytes 1048592 | tf_op jit(solution)/shard_map/psum | solution.py:53
  123.4 143.1 %all-reduce.9.cloned.1.call-done = bf16[512,3072]{1,0:T(8,128)(2,1)} async-done(((bf16[512,3072]{1,0:T(8,128)(2,1)}), bf16[512,3072]{1,0:T(8,128)(2,1)}) %all-reduce.9.cloned.1.call-update) | async-done | bytes 3145744 | tf_op jit(solution)/shard_map/psum | solution.py:15
  266.5 42.6 %fusion.12 = f32[512,512]{0,1:T(8,128)S(1)} fusion(bf16[512,3072]{1,0:T(8,128)(2,1)} %all-reduce.9.cloned.1.call-done, f32[3072]{0:T(1024)S(1)} %fusion.39, f32[512,512]{0,1:T(8,128)} %all-reduce.11.cloned.1.call-done, f32[512]{0:T(512)S(1)} %multiply_add_fusion), kind=kOutput, calls=%fused_computation.22 | convolution fusion | flops 9685434368 | bytes 5257216 | tf_op jit(solution)/shard_map/dot_general | solution.py:79
  309.1 0.3 copy.11
  309.4 0.2 fusion.19
  309.7 11.7 %cholesky.104 = f32[128,128]{1,0:T(8,128)S(1)} custom-call(f32[128,128]{1,0:T(8,128)S(1)} %cholesky.266), custom_call_target="Cholesky" | custom-call | tf_op jit(solution)/shard_map/jit(cholesky)/cholesky | solution.py:85
  321.4 0.1 cholesky.224
  321.6 9.8 %custom-call.30 = f32[1,128,128]{1,2,0:T(8,128)S(1)} custom-call(f32[1,128,128]{2,1,0:T(8,128)S(1)} %get-tuple-element.34), custom_call_target="InvertDiagBlocksLowerTriangular" | custom-call | tf_op jit(solution)/shard_map/jit(cholesky)/cholesky | solution.py:85
  331.4 0.3 constant_dynamic-update-slice_fusion.3
  331.7 0.3 convolution_subtract_fusion.2
  332.0 11.7 %cholesky.217 = f32[128,128]{1,0:T(8,128)S(1)} custom-call(f32[128,128]{1,0:T(8,128)S(1)} %cholesky.270), custom_call_target="Cholesky" | custom-call | tf_op jit(solution)/shard_map/jit(cholesky)/cholesky | solution.py:85
  343.8 10.0 %custom-call.31 = f32[1,128,128]{1,2,0:T(8,128)S(1)} custom-call(f32[1,128,128]{2,1,0:T(8,128)S(1)} %get-tuple-element.31), custom_call_target="InvertDiagBlocksLowerTriangular" | custom-call | tf_op jit(solution)/shard_map/jit(cholesky)/cholesky | solution.py:85
  353.8 0.3 convolution_dynamic-update-slice_fusion
  354.0 0.4 convolution_subtract_fusion.3
  354.4 11.7 %cholesky.238 = f32[128,128]{1,0:T(8,128)S(1)} custom-call(f32[128,128]{1,0:T(8,128)S(1)} %cholesky.275), custom_call_target="Cholesky" | custom-call | tf_op jit(solution)/shard_map/jit(cholesky)/cholesky | solution.py:85
  366.2 9.8 %custom-call.32 = f32[1,128,128]{1,2,0:T(8,128)S(1)} custom-call(f32[1,128,128]{2,1,0:T(8,128)S(1)} %get-tuple-element.28), custom_call_target="InvertDiagBlocksLowerTriangular" | custom-call | tf_op jit(solution)/shard_map/jit(cholesky)/cholesky | solution.py:85
  376.0 0.2 convolution_dynamic-update-slice_fusion.1
  376.2 0.4 convolution_subtract_fusion.4
  376.6 11.7 %cholesky.255 = f32[128,128]{1,0:T(8,128)S(1)} custom-call(f32[128,128]{1,0:T(8,128)S(1)} %convolution_subtract_fusion.4), custom_call_target="Cholesky" | custom-call | tf_op jit(solution)/shard_map/jit(cholesky)/cholesky | solution.py:85
  388.3 0.6 compare_reduce_fusion.2
  390.2 0.6 compare_reduce_fusion.1
  391.5 0.6 compare_reduce_fusion
  392.8 0.1 select_select_fusion
  392.9 7.7 %while.1 = (s32[]{:T(128)}, f32[512,512]{1,0:T(8,128)S(1)}, s32[4,2]{0,1:T(2,128)S(1)}, f32[4,128,128]{2,1,0:T(8,128)S(1)}, s32[]{:T(128)}) while((s32[]{:T(128)}, f32[512,512]{1,0:T(8,128)S(1)}, s32[4,2]{0,1:T(2,128)S(1)}, f32[4,128,128]{2,1,0:T(8,128)S(1)}, s32[]{:T(128)}) %tuple.27), condition=%wide.while_cond, body=%wide.while_body.sunk | while | flops 2 | bytes 131189 | solution.py:86
  392.9 0.1 constant_dynamic-slice_fusion.2
  393.0 0.5 fusion.58
  393.5 1.3 bitcast_dynamic-update-slice_fusion.2
  394.8 0.1 constant_dynamic-slice_fusion.2
  394.9 0.5 fusion.58
  395.4 1.3 bitcast_dynamic-update-slice_fusion.2
  396.8 0.1 constant_dynamic-slice_fusion.2
  396.8 0.5 fusion.58
  397.4 1.3 bitcast_dynamic-update-slice_fusion.2
  398.7 0.1 constant_dynamic-slice_fusion.2
  398.8 0.5 fusion.58
  399.3 1.3 bitcast_dynamic-update-slice_fusion.2
  400.6 39.3 %custom-call.33 = f32[4,128,128]{1,2,0:T(8,128)S(1)} custom-call(f32[4,128,128]{2,1,0:T(8,128)S(1)} %get-tuple-element.12), custom_call_target="InvertDiagBlocksLowerTriangular" | custom-call | tf_op jit(solution)/shard_map/triangular_solve | solution.py:86
  439.9 5.4 %convert_multiply_fusion.9 = f32[512,3072]{1,0:T(8,128)} fusion(bf16[512,3072]{1,0:T(8,128)(2,1)} %all-reduce.9.cloned.1.call-done, f32[3072]{0:T(1024)S(1)} %fusion.39), kind=kLoop, calls=%fused_computation.4.clone.1.clone.clone.clone.1 | loop fusion | flops 3145728 | bytes 9449472 | tf_op jit(solution)/shard_map/dot_general | solution.py:71
  445.4 81.9 %fusion.5 = f32[1024,512]{0,1:T(8,128)S(1)} fusion(f32[1024,512]{0,1:T(8,128)} %reduce-scatter.2.cloned.1.call-done, f32[1024,3072]{1,0:T(8,128)} %param.5, f32[512]{0:T(512)S(1)} %multiply_add_fusion, f32[1024]{0:T(1024)S(1)} %fusion.40, s32[1024]{0:T(1024)S(1)} %iota_add_fusion, s32[512]{0:T(512)S(1)} %iota_add_fusion.1, ...), kind=kOutput, calls=%fused_computation.12 | convolution fusion | flops 19364577280 | bytes 23080960 | tf_op jit(solution)/shard_map/dot_general | solution.py:71
  527.3 0.6 fusion.20
  527.9 0.6 convolution_subtract_fusion.1
  528.5 0.6 fusion.32
  529.2 0.7 convolution_subtract_fusion
  529.9 0.6 fusion.31
  530.5 1.2 fusion.13
  531.7 0.6 fusion.30
  532.3 0.1 pad_maximum_fusion
  532.4 1.8 copy.12
  (21 shorter events, 0.2 us)
Async XLA Ops:
  6.5 62.4 %all-reduce.7.cloned.1.call-start = ((), (), s32[]{:S(2)}) async-start(), calls=%async_computation.1 | async-start | bytes 1572864 | tf_op jit(solution)/shard_map/psum | solution.py:15
  9.4 114.0 %all-reduce.11.cloned.1.call-start = ((), (), s32[]{:S(2)}) async-start(), calls=%async_computation.4 | async-start | bytes 2097152 | tf_op jit(solution)/shard_map/psum | solution.py:53
  71.9 194.6 %all-reduce.9.cloned.1.call-start = ((), (), s32[]{:S(2)}) async-start(), calls=%async_computation.3 | async-start | bytes 6291456 | tf_op jit(solution)/shard_map/psum | solution.py:15
  77.2 1.1 copy-start
  77.3 368.1 %reduce-scatter.2.cloned.1.call-start = ((), (), s32[]{:S(2)}) async-start(), calls=%async_computation.2 | async-start | bytes 10485760 | tf_op jit(solution)/shard_map/reduce_scatter | solution.py:60
  86.8 0.7 copy-start.1
Sparse Core Ops, SparseCore 0:
  10.5 58.3 all-reduce.6
  72.0 51.3 all-reduce.10
  128.9 137.5 all-reduce.8
  268.7 143.3 reduce-scatter.1
where the time goes:
time: 545 us; the launch traced here: 541 us
  waiting for transfers between devices  213 us (39%)
  matrix products  143 us (26%)
  other arithmetic  136 us (25%)
  blocking collectives  19.6 us (4%)
  between operations  18.2 us (3%)
  local copies, waits for them, and re-layouts  11.6 us (2%)
    psum x2, waiting for transfers between devices, from_root(): return lax.psum(jnp.where(mine, shard, jnp.zeros_like(shard)), axis)  203 us
    dot_general x1, matrix products, body(): jnp.dot(factor, panel_rows.T, precision=lax.Precision.HIGHEST, preferred_...  81.9 us
    another operation x14, other arithmetic, body(): lower_factor = jnp.linalg.cholesky(diag_block)  78.5 us
    dot_general x1, matrix products, body(): jnp.dot(panel_rows, panel_rows.T, precision=lax.Precision.HIGHEST, prefer...  42.6 us
    another operation x4, other arithmetic, body(): lax.linalg.triangular_solve(lower_factor, updated, left_side=False, lower...  39.6 us
    psum x1, blocking collectives, body(): pair_sum, panel_sum = lax.psum((pair_part, panel_part), ('fac', 'pair'))  19.6 us
  transfers between devices with their start and end apart: 4, of which 3 were waited for; matrix products, arithmetic and copies ran while one was open for 36% of the time, Pallas kernels for 0%

commit v1 on v0

--- a/solution.py
+++ b/solution.py
@@ -50,7 +50,7 @@
     pair_part = lax.dot_general(
         panel_points, panel_points, (((1,), (1,)), ((), ())), preferred_element_type=jnp.float32
     )
-    pair_sum, panel_sum = lax.psum((pair_part, panel_part), ("fac", "pair"))
+    pair_sum, panel_sum = lax.psum(lax.psum((pair_part, panel_part), "pair"), "fac")
     panel_norm = panel_sum / DIN + EPS
     row_part = jnp.sum(jnp.square(points.astype(jnp.float32)), axis=1)
     inner_part = lax.dot_general(

time: 545 us -> 595 us (1.092)
  waiting for transfers between devices: 213 us -> 253 us
  blocking collectives: 19.6 us -> 29.3 us
    psum x1 -> x2, waiting for transfers between devices: 10.6 us -> 94.2 us  [the longest x1 59.5 us: body(): lax.psum(lax.psum((pair_part, panel_part), 'pair'), 'fac')]
    psum x2, waiting for transfers between devices: 203 us -> 159 us  [from_root(): return lax.psum(jnp.where(mine, shard, jnp.zeros_like(shard)), axis)]
    unnamed x0 -> x1, blocking collectives: none -> 18.5 us
    psum x1 -> x2, blocking collectives: 19.6 us -> 10.7 us  [the longest x1 5.81 us: body(): lax.psum(lax.psum((pair_part, panel_part), 'pair'), 'fac')]
  transfers between devices with their start and end apart: 4 -> 5, of which waited for: 3 -> 4; matrix products, arithmetic and copies ran while one was open for 36% -> 33% of each run, Pallas kernels for 0% -> 0%
where the time goes in v1:
time: 595 us; the launch traced here: 590 us
  waiting for transfers between devices  253 us (43%)
  matrix products  143 us (24%)
  other arithmetic  136 us (23%)
  blocking collectives  29.3 us (5%)
  between operations  18.2 us (3%)
  local copies, waits for them, and re-layouts  10.7 us (2%)
    psum x2, waiting for transfers between devices, from_root(): return lax.psum(jnp.where(mine, shard, jnp.zeros_like(shard)), axis)  159 us
    dot_general x1, matrix products, body(): jnp.dot(factor, panel_rows.T, precision=lax.Precision.HIGHEST, preferred_...  82 us
    another operation x14, other arithmetic, body(): lower_factor = jnp.linalg.cholesky(diag_block)  78.5 us
    psum x1, waiting for transfers between devices, body(): lax.psum(lax.psum((pair_part, panel_part), 'pair'), 'fac')  59.5 us
    dot_general x1, matrix products, body(): jnp.dot(panel_rows, panel_rows.T, precision=lax.Precision.HIGHEST, prefer...  42.5 us
    another operation x4, other arithmetic, body(): lax.linalg.triangular_solve(lower_factor, updated, left_side=False, lower...  39.6 us
    psum x1, waiting for transfers between devices, body(): lax.psum((pair_part, panel_part), 'pair')  34.7 us
    unnamed x1, blocking collectives  18.5 us
  transfers between devices with their start and end apart: 5, of which 4 were waited for; matrix products, arithmetic and copies ran while one was open for 33% of the time, Pallas kernels for 0%

profile of v1, /device:TPU:0, one launch (start us, length us, event | category | flops | bytes accessed | tf_op | source)
XLA Modules:
  0.0 590.0 jit_solution(3684970004734371496)
XLA Ops:
  7.2 2.1 dynamic-slice_select_fusion
  9.4 0.0 all-reduce.11.cloned.1.call-start
  9.4 59.5 %all-reduce.7.cloned.1.call-done = bf16[512,768]{1,0:T(8,128)(2,1)} async-done(((bf16[512,768]{1,0:T(8,128)(2,1)}), bf16[512,768]{1,0:T(8,128)(2,1)}) %all-reduce.7.cloned.1.call-update) | async-done | bytes 786448 | tf_op jit(solution)/shard_map/psum | solution.py:15
  68.9 2.9 fusion.44
  71.9 0.0 all-reduce.9.cloned.1.call-start
  72.0 5.3 fusion.2
  77.2 0.0 all-reduce.13.cloned.1.call-start
  77.3 34.7 %all-reduce.11.cloned.1.call-done = f32[512,512]{0,1:T(8,128)} async-done(((f32[512,512]{0,1:T(8,128)}), f32[512,512]{0,1:T(8,128)}) %all-reduce.11.cloned.1.call-update) | async-done | bytes 1048592 | tf_op jit(solution)/shard_map/psum | solution.py:53
  112.0 0.0 reduce-scatter.2.cloned.1.call-start
  112.1 8.4 %convolution_bitcast_fusion = f32[4096,512]{0,1:T(8,128)} fusion(bf16[512,768]{1,0:T(8,128)(2,1)S(1)} %copy-done, bf16[4096,768]{1,0:T(8,128)(2,1)} %param.4), kind=kOutput, calls=%fused_computation.3 | convolution fusion | flops 3221225472 | bytes 15466496 | tf_op jit(solution)/shard_map/dot_general | solution.py:56
  121.2 0.6 dynamic-slice.3
  122.5 4.2 multiply_reduce_fusion
  126.7 18.5 %all-reduce.1 = f32[4096]{0:T(1024)S(1)} all-reduce(f32[4096]{0:T(1024)S(1)} %multiply_reduce_fusion), channel_id=2, replica_groups=mesh['kern'=8,'fac'=2,'pair'=2] {'fac','pair'}, use_global_device_ids=true, to_apply=%region_1.2.clone | all-reduce | flops 4096 | bytes 32768
  145.3 0.2 multiply_reduce_fusion.1
  145.5 4.9 psum.43
  150.5 5.8 psum.44
  156.3 99.4 %all-reduce.9.cloned.1.call-done = bf16[512,3072]{1,0:T(8,128)(2,1)} async-done(((bf16[512,3072]{1,0:T(8,128)(2,1)}), bf16[512,3072]{1,0:T(8,128)(2,1)}) %all-reduce.9.cloned.1.call-update) | async-done | bytes 3145744 | tf_op jit(solution)/shard_map/psum | solution.py:15
  255.7 5.4 convert_multiply_fusion.9
  261.1 59.5 %all-reduce.13.cloned.1.call-done = f32[512,512]{0,1:T(8,128)} async-done(((f32[512,512]{0,1:T(8,128)}), f32[512,512]{0,1:T(8,128)}) %all-reduce.13.cloned.1.call-update) | async-done | bytes 1048592 | tf_op jit(solution)/shard_map/psum | solution.py:53
  320.6 42.5 %fusion.12 = f32[512,512]{0,1:T(8,128)S(1)} fusion(bf16[512,3072]{1,0:T(8,128)(2,1)} %all-reduce.9.cloned.1.call-done, f32[3072]{0:T(1024)S(1)} %fusion.39, f32[512,512]{0,1:T(8,128)} %all-reduce.13.cloned.1.call-done, f32[512]{0:T(512)S(1)} %multiply_add_fusion), kind=kOutput, calls=%fused_computation.22 | convolution fusion | flops 9685434368 | bytes 5257216 | tf_op jit(solution)/shard_map/dot_general | solution.py:79
  363.2 0.3 copy.11
  363.5 0.2 fusion.19
  363.8 11.7 %cholesky.104 = f32[128,128]{1,0:T(8,128)S(1)} custom-call(f32[128,128]{1,0:T(8,128)S(1)} %cholesky.266), custom_call_target="Cholesky" | custom-call | tf_op jit(solution)/shard_map/jit(cholesky)/cholesky | solution.py:85
  375.5 0.1 cholesky.224
  375.7 9.8 %custom-call.30 = f32[1,128,128]{1,2,0:T(8,128)S(1)} custom-call(f32[1,128,128]{2,1,0:T(8,128)S(1)} %get-tuple-element.32), custom_call_target="InvertDiagBlocksLowerTriangular" | custom-call | tf_op jit(solution)/shard_map/jit(cholesky)/cholesky | solution.py:85
  385.5 0.3 constant_dynamic-update-slice_fusion.3
  385.8 0.3 convolution_subtract_fusion.2
  386.1 11.7 %cholesky.217 = f32[128,128]{1,0:T(8,128)S(1)} custom-call(f32[128,128]{1,0:T(8,128)S(1)} %cholesky.270), custom_call_target="Cholesky" | custom-call | tf_op jit(solution)/shard_map/jit(cholesky)/cholesky | solution.py:85
  397.9 10.0 %custom-call.31 = f32[1,128,128]{1,2,0:T(8,128)S(1)} custom-call(f32[1,128,128]{2,1,0:T(8,128)S(1)} %get-tuple-element.29), custom_call_target="InvertDiagBlocksLowerTriangular" | custom-call | tf_op jit(solution)/shard_map/jit(cholesky)/cholesky | solution.py:85
  407.9 0.3 convolution_dynamic-update-slice_fusion
  408.1 0.4 convolution_subtract_fusion.3
  408.5 11.7 %cholesky.238 = f32[128,128]{1,0:T(8,128)S(1)} custom-call(f32[128,128]{1,0:T(8,128)S(1)} %cholesky.275), custom_call_target="Cholesky" | custom-call | tf_op jit(solution)/shard_map/jit(cholesky)/cholesky | solution.py:85
  420.3 9.8 %custom-call.32 = f32[1,128,128]{1,2,0:T(8,128)S(1)} custom-call(f32[1,128,128]{2,1,0:T(8,128)S(1)} %get-tuple-element.26), custom_call_target="InvertDiagBlocksLowerTriangular" | custom-call | tf_op jit(solution)/shard_map/jit(cholesky)/cholesky | solution.py:85
  430.1 0.2 convolution_dynamic-update-slice_fusion.1
  430.3 0.4 convolution_subtract_fusion.4
  430.7 11.7 %cholesky.255 = f32[128,128]{1,0:T(8,128)S(1)} custom-call(f32[128,128]{1,0:T(8,128)S(1)} %convolution_subtract_fusion.4), custom_call_target="Cholesky" | custom-call | tf_op jit(solution)/shard_map/jit(cholesky)/cholesky | solution.py:85
  442.4 0.7 compare_reduce_fusion.2
  444.3 0.6 compare_reduce_fusion.1
  445.6 0.6 compare_reduce_fusion
  446.9 0.1 select_select_fusion
  447.1 7.9 %while.1 = (s32[]{:T(128)}, f32[512,512]{1,0:T(8,128)S(1)}, s32[4,2]{0,1:T(2,128)S(1)}, f32[4,128,128]{2,1,0:T(8,128)S(1)}, s32[]{:T(128)}) while((s32[]{:T(128)}, f32[512,512]{1,0:T(8,128)S(1)}, s32[4,2]{0,1:T(2,128)S(1)}, f32[4,128,128]{2,1,0:T(8,128)S(1)}, s32[]{:T(128)}) %tuple.27), condition=%wide.while_cond, body=%wide.while_body.sunk | while | flops 2 | bytes 131189 | solution.py:86
  447.1 0.1 constant_dynamic-slice_fusion.2
  447.2 0.5 fusion.58
  447.7 1.4 bitcast_dynamic-update-slice_fusion.2
  449.1 0.1 constant_dynamic-slice_fusion.2
  449.1 0.5 fusion.58
  449.7 1.4 bitcast_dynamic-update-slice_fusion.2
  451.1 0.1 constant_dynamic-slice_fusion.2
  451.1 0.5 fusion.58
  451.7 1.4 bitcast_dynamic-update-slice_fusion.2
  453.0 0.1 constant_dynamic-slice_fusion.2
  453.1 0.5 fusion.58
  453.6 1.4 bitcast_dynamic-update-slice_fusion.2
  455.0 39.3 %custom-call.33 = f32[4,128,128]{1,2,0:T(8,128)S(1)} custom-call(f32[4,128,128]{2,1,0:T(8,128)S(1)} %get-tuple-element.12), custom_call_target="InvertDiagBlocksLowerTriangular" | custom-call | tf_op jit(solution)/shard_map/triangular_solve | solution.py:86
  494.4 82.0 %fusion.5 = f32[1024,512]{0,1:T(8,128)S(1)} fusion(f32[1024,512]{0,1:T(8,128)} %reduce-scatter.2.cloned.1.call-done, f32[1024,3072]{1,0:T(8,128)} %param.5, f32[512]{0:T(512)S(1)} %multiply_add_fusion, f32[1024]{0:T(1024)S(1)} %fusion.40, s32[1024]{0:T(1024)S(1)} %iota_add_fusion, s32[512]{0:T(512)S(1)} %iota_add_fusion.1, ...), kind=kOutput, calls=%fused_computation.12 | convolution fusion | flops 19364577280 | bytes 23080960 | tf_op jit(solution)/shard_map/dot_general | solution.py:71
  576.3 0.6 fusion.20
  576.9 0.6 convolution_subtract_fusion.1
  577.6 0.6 fusion.32
  578.2 0.7 convolution_subtract_fusion
  578.9 0.6 fusion.31
  579.5 1.2 fusion.13
  580.7 0.6 fusion.30
  581.3 0.1 pad_maximum_fusion
  581.5 1.8 copy.12
  (26 shorter events, 0.3 us)
Async XLA Ops:
  6.5 62.4 %all-reduce.7.cloned.1.call-start = ((), (), s32[]{:S(2)}) async-start(), calls=%async_computation.1 | async-start | bytes 1572864 | tf_op jit(solution)/shard_map/psum | solution.py:15
  9.4 102.6 %all-reduce.11.cloned.1.call-start = ((), (), s32[]{:S(2)}) async-start(), calls=%async_computation.4 | async-start | bytes 2097152 | tf_op jit(solution)/shard_map/psum | solution.py:53
  71.9 183.8 %all-reduce.9.cloned.1.call-start = ((), (), s32[]{:S(2)}) async-start(), calls=%async_computation.3 | async-start | bytes 6291456 | tf_op jit(solution)/shard_map/psum | solution.py:15
  77.2 34.9 %copy-start = (bf16[512,768]{1,0:T(8,128)(2,1)S(1)}, bf16[512,768]{1,0:T(8,128)(2,1)}, u32[]{:S(2)}) copy-start(bf16[512,768]{1,0:T(8,128)(2,1)} %all-reduce.7.cloned.1.call-done) | copy-start | bytes 2359300
  77.2 243.4 %all-reduce.13.cloned.1.call-start = ((), (), s32[]{:S(2)}) async-start(), calls=%async_computation.5 | async-start | bytes 2097152 | tf_op jit(solution)/shard_map/psum | solution.py:53
  112.0 382.3 %reduce-scatter.2.cloned.1.call-start = ((), (), s32[]{:S(2)}) async-start(), calls=%async_computation.2 | async-start | bytes 10485760 | tf_op jit(solution)/shard_map/reduce_scatter | solution.py:60
  120.5 0.7 copy-start.1
Sparse Core Ops, SparseCore 0:
  10.5 58.3 all-reduce.6
  72.0 39.9 all-reduce.10
  117.5 138.1 all-reduce.8
  257.9 62.7 all-reduce.12
  322.8 143.6 reduce-scatter.1
